TPU v7x, 256 devices: a whole 4x4x8 slice. The times are simulated.
256 devices in a mesh: seq: 64 (over z, x, core), fsdp: 4 (over y).
Axes of the slice: x: 4, y: 4, z: 8, core: 2. Of those that a mesh axis runs over, the one named last changes fastest.
Arguments:
- query_rows: bfloat16 [32768, 4096], P('seq', 'fsdp'), may hold values from -6 to 6
- key_rows: bfloat16 [32768, 4096], P('seq', 'fsdp'), may hold values from -0.5390625 to 0.5390625
- value_rows: bfloat16 [32768, 4096], P('seq', 'fsdp'), may hold values from -6 to 6
- norm_gain: float32 [4096], P('fsdp'), may hold values from 0.1 to 1.9
- out_weight: bfloat16 [4096, 4096], P(None, 'fsdp'), may hold values from -0.09375 to 0.09375
Outputs:
- mixed: bfloat16 [32768, 4096], P('seq', 'fsdp')
All inputs are finite; a program needn't handle non-finite values.
Results may differ from a plain program's by a relative error of at most 0.012.
Values may be sent and summed in bfloat16 or wider, within the bound.
No kernel may reach another device: no remote copies, remote signals or barrier semaphores. Data moves between devices by JAX's collectives and lax.ppermute only.
A program may use at most 192 MiB of HBM per device.

v0:
```python
import jax
import jax.numpy as jnp
from jax import lax
from jax.sharding import PartitionSpec as P

DH = 128
BLK = 512


def entering(value, axis, combine, identity):
    count, index = (lax.axis_size(axis), lax.axis_index(axis))
    everything = lax.all_gather(value, axis)
    start = jnp.broadcast_to(jnp.asarray(identity, value.dtype), value.shape)

    def step(k, before):
        reached = k < index
        new = combine(before, everything[k])
        return jnp.where(reached, new, before)

    return lax.fori_loop(0, count, step, start)


def add_states(earlier, later):
    return earlier + later


def earlier_states(local_total):
    return entering(local_total, "seq", add_states, jnp.zeros_like(local_total))


def shards(query_rows, key_rows, value_rows, norm_gain, out_weight):
    tokens = query_rows.shape[0]
    feature_width = query_rows.shape[1]
    heads_here = feature_width // DH
    n_blocks = tokens // BLK
    highest = lax.Precision.HIGHEST
    queries_b = query_rows.reshape(n_blocks, BLK, heads_here, DH)
    keys_b = key_rows.reshape(n_blocks, BLK, heads_here, DH)
    values_b = value_rows.reshape(n_blocks, BLK, heads_here, DH)
    block_state = jnp.einsum(
        "nkhd,nkhe->nhde", keys_b, values_b, preferred_element_type=jnp.float32
    )
    local_total = jnp.sum(block_state, axis=0)
    running_sum = jnp.cumsum(block_state, axis=0)
    local_before = jnp.concatenate([jnp.zeros_like(block_state), running_sum[:-1]], axis=0)
    position = lax.broadcasted_iota(jnp.int32, (BLK, BLK), 0)
    column = lax.broadcasted_iota(jnp.int32, (BLK, BLK), 1)
    causal_mask = column <= position
    queries_f = queries_b.astype(jnp.float32)
    prefix = earlier_states(local_total)
    carried = prefix[None] + local_before
    from_state = jnp.einsum("nqhd,nhde->nqhe", queries_f, carried, precision=highest)
    scores = jnp.einsum("nqhd,nkhd->nhqk", queries_b, keys_b, preferred_element_type=jnp.float32)
    masked_scores = jnp.where(causal_mask[None, None], scores, 0.0).astype(jnp.bfloat16)
    attention = (
        jnp.einsum("nhqk,nkhd->nqhd", masked_scores, values_b, preferred_element_type=jnp.float32)
        + from_state
    )
    mean_square = jnp.mean(attention * attention, axis=-1, keepdims=True)
    normed = attention * lax.rsqrt(mean_square + 1e-06) * norm_gain.reshape(heads_here, DH)
    normed = normed.astype(jnp.bfloat16).reshape(tokens, feature_width)
    summed = jnp.dot(
        lax.all_gather(normed, "fsdp", axis=1, tiled=True),
        out_weight,
        preferred_element_type=jnp.float32,
    )
    return summed.astype(jnp.bfloat16)


def solution(mesh):
    placed = (P("seq", "fsdp"), P("seq", "fsdp"), P("seq", "fsdp"), P("fsdp"), P(None, "fsdp"))
    return jax.shard_map(
        shards, mesh=mesh, in_specs=placed, out_specs=P("seq", "fsdp"), check_vma=False
    )
```

profile of v0, /device:TPU:1, one launch (start us, length us, event | category | flops | bytes accessed | tf_op | source)
XLA Modules:
  0.0 313.3 jit_solution(7516923831967842303)
XLA Ops:
  6.5 1.6 copy.17
  8.1 2.5 fusion.9
  10.8 146.7 %all-gather.6.cloned.1.call-done = f32[512,128,128]{2,1,0:T(8,128)} async-done(((f32[8,128,128]{2,1,0:T(8,128)}), f32[512,128,128]{2,1,0:T(8,128)}) %all-gather.6.cloned.1.call-update) | async-done | bytes 33554448 | tf_op jit(solution)/shard_map/all_gather | solution.py:12
  157.5 80.1 %while.14 = (s32[]{:T(128)}, f32[8,128,128]{2,1,0:T(8,128)S(1)}, s32[]{:T(128)}, f32[64,8,128,128]{3,2,1,0:T(8,128)}, s32[]{:T(128)}, /*index=5*/s32[]{:T(128)}) while((s32[]{:T(128)}, f32[8,128,128]{2,1,0:T(8,128)S(1)}, s32[]{:T(128)}, f32[64,8,128,128]{3,2,1,0:T(8,128)}, s32[]{:T(128)}, /*index=5*/s32[]{:T(128)}) %tuple.40), condition=%wide.region_1.0_spmd.clone, body=%wide.region_0.0_spmd.clone.sunk | while | flops 393220 | bytes 1572957 | solution.py:20
  158.7 1.2 add_select_fusion.2
  160.0 1.2 add_select_fusion.2
  161.2 1.2 add_select_fusion.2
  162.5 1.2 add_select_fusion.2
  163.7 1.2 add_select_fusion.2
  165.0 1.2 add_select_fusion.2
  166.2 1.2 add_select_fusion.2
  167.5 1.2 add_select_fusion.2
  168.7 1.2 add_select_fusion.2
  171.2 1.2 add_select_fusion.2
  172.5 1.2 add_select_fusion.2
  195.0 1.2 add_select_fusion.2
  196.3 1.2 add_select_fusion.2
  218.8 1.2 add_select_fusion.2
  220.1 1.2 add_select_fusion.2
  237.6 2.4 fusion.13
  240.0 5.9 %fusion.5 = (f32[512,8]{0,1:T(8,128)S(1)}, f32[8,128,512]{2,1,0:T(8,128)}) fusion(f32[8,128,512]{2,1,0:T(8,128)} %fusion.13, pred[512,512]{1,0:T(8,128)(4,1)S(1)} %iota_compare_fusion, bf16[512,8,128]{0,2,1:T(8,128)(2,1)S(1)} %bitcast.57, bf16[512,1024]{1,0:T(8,128)(2,1)} %param.9, bf16[512,1024]{1,0:T(8,128)(2,1)S(1)} %copy-done), kind=kOutput, calls=%fused_computation.8 | convolution fusion | flops 1079504896 | bytes 7618560 | tf_op jit(solution)/shard_map/nhqk,nkhd->nqhd/dot_general | solution.py:56
  245.9 2.8 fusion.7
  248.7 47.6 %all-gather.4.cloned.1.call-done = bf16[512,4096]{0,1:T(8,128)(2,1)} async-done(((bf16[512,1024]{0,1:T(8,128)(2,1)}), bf16[512,4096]{0,1:T(8,128)(2,1)}) %all-gather.4.cloned.1.call-update) | async-done | bytes 4194320 | tf_op jit(solution)/shard_map/all_gather | solution.py:63
  296.3 10.1 %convolution_convert_fusion = bf16[512,1024]{1,0:T(8,128)(2,1)} fusion(bf16[512,4096]{0,1:T(8,128)(2,1)} %all-gather.4.cloned.1.call-done, bf16[4096,1024]{1,0:T(8,128)(2,1)} %param.11), kind=kOutput, calls=%fused_computation.12 | convolution fusion | flops 4295491584 | bytes 13631488 | tf_op jit(solution)/shard_map/dot_general | solution.py:62
  (60 shorter events, 60.3 us)
Async XLA Ops:
  6.5 231.0 %copy-start = (bf16[512,1024]{1,0:T(8,128)(2,1)S(1)}, bf16[512,1024]{1,0:T(8,128)(2,1)}, u32[]{:S(2)}) copy-start(bf16[512,1024]{1,0:T(8,128)(2,1)} %param.7) | copy-start | bytes 3145732
  6.5 150.9 %all-gather.6.cloned.1.call-start = ((), (), s32[]{:S(2)}) async-start(), calls=%async_computation.1 | async-start | bytes 34078720 | tf_op jit(solution)/shard_map/all_gather | solution.py:12
  10.6 285.7 %all-gather.4.cloned.1.call-start = ((), (), s32[]{:S(2)}) async-start(), calls=%async_computation | async-start | bytes 5242880 | tf_op jit(solution)/shard_map/all_gather | solution.py:63
  240.0 5.9 %copy-start.1 = (f32[1024]{0:T(1024)S(1)}, f32[1024]{0:T(1024)}, u32[]{:S(2)}) copy-start(f32[1024]{0:T(1024)} %param.10) | copy-start | bytes 12292
Sparse Core Ops, SparseCore 0:
  10.7 146.6 all-gather.5
  248.8 47.4 all-gather.3
where the time goes:
time: 317 us; the launch traced here: 313 us
  waiting for transfers between devices  194 us (61%)
  other arithmetic  81.4 us (26%)
  matrix products  20.9 us (7%)
  between operations  13.5 us (4%)
    all_gather x1, waiting for transfers between devices, entering(): everything = lax.all_gather(value, axis)  147 us
    select_n x64, other arithmetic, step(): return jnp.where(reached, new, before)  78.5 us
    all_gather x1, waiting for transfers between devices, shards(): lax.all_gather(normed, 'fsdp', axis=1, tiled=True)  47.6 us
    dot_general x1, matrix products, shards(): jnp.dot(lax.all_gather(normed, 'fsdp', axis=1, tiled=True), out_weight, p...  10.1 us
  transfers between devices with their start and end apart: 2, of which 2 were waited for; matrix products, arithmetic and copies ran while one was open for 0% of the time, Pallas kernels for 0%

commit v1 on v0

--- a/solution.py
+++ b/solution.py
@@ -5,6 +5,14 @@
 
 DH = 128
 BLK = 512
+
+
+def tiled_gather(array, axis, dim):
+    count = lax.axis_size(axis)
+    repeats = [count if d == dim else 1 for d in range(array.ndim)]
+    return lax.all_to_all(
+        jnp.tile(array, repeats), axis, split_axis=dim, concat_axis=dim, tiled=True
+    )
 
 
 def entering(value, axis, combine, identity):
@@ -60,9 +68,7 @@
     normed = attention * lax.rsqrt(mean_square + 1e-06) * norm_gain.reshape(heads_here, DH)
     normed = normed.astype(jnp.bfloat16).reshape(tokens, feature_width)
     summed = jnp.dot(
-        lax.all_gather(normed, "fsdp", axis=1, tiled=True),
-        out_weight,
-        preferred_element_type=jnp.float32,
+        tiled_gather(normed, "fsdp", 1), out_weight, preferred_element_type=jnp.float32
     )
     return summed.astype(jnp.bfloat16)
 

time: 317 us -> 328 us (1.035)
  blocking collectives: 0 us -> 52.3 us
  waiting for transfers between devices: 194 us -> 147 us
  local copies, waits for them, and re-layouts: 1.59 us -> 8.9 us
    all_to_all x0 -> x1, blocking collectives: none -> 52.3 us  [tiled_gather(): lax.all_to_all(jnp.tile(array, repeats), axis, split_axis=dim, concat_axi...]
    all_gather x1 -> x0, waiting for transfers between devices: 47.6 us -> none  [shards(): lax.all_gather(normed, 'fsdp', axis=1, tiled=True)]
    all_to_all x0 -> x1, local copies, waits for them, and re-layouts: none -> 6.25 us  [tiled_gather(): lax.all_to_all(jnp.tile(array, repeats), axis, split_axis=dim, concat_axi...]
  transfers between devices with their start and end apart: 2 -> 1, of which waited for: 2 -> 1; matrix products, arithmetic and copies ran while one was open for 0% -> 0% of each run, Pallas kernels for 0% -> 0%
where the time goes in v1:
time: 328 us; the launch traced here: 324 us
  waiting for transfers between devices  147 us (45%)
  other arithmetic  80.5 us (25%)
  blocking collectives  52.3 us (16%)
  matrix products  20.9 us (6%)
  between operations  13.5 us (4%)
  local copies, waits for them, and re-layouts  8.9 us (3%)
    all_gather x1, waiting for transfers between devices, entering(): everything = lax.all_gather(value, axis)  147 us
    select_n x64, other arithmetic, step(): return jnp.where(reached, new, before)  78.5 us
    all_to_all x1, blocking collectives, tiled_gather(): lax.all_to_all(jnp.tile(array, repeats), axis, split_axis=dim, concat_axi...  52.3 us
    dot_general x1, matrix products, shards(): jnp.dot(tiled_gather(normed, 'fsdp', 1), out_weight, preferred_element_ty...  10.2 us
  transfers between devices with their start and end apart: 1, of which 1 were waited for; matrix products, arithmetic and copies ran while one was open for 0% of the time, Pallas kernels for 0%

profile of v1, /device:TPU:1, one launch (start us, length us, event | category | flops | bytes accessed | tf_op | source)
XLA Modules:
  0.0 324.4 jit_solution(1492692982043100559)
XLA Ops:
  6.5 1.6 copy.28
  8.1 2.5 fusion.9
  10.7 146.8 %all-gather.3.cloned.1.call-done = f32[512,128,128]{2,1,0:T(8,128)} async-done(((f32[8,128,128]{2,1,0:T(8,128)}), f32[512,128,128]{2,1,0:T(8,128)}) %all-gather.3.cloned.1.call-update) | async-done | bytes 33554448 | tf_op jit(solution)/shard_map/all_gather | solution.py:20
  157.5 80.1 %while.14 = (s32[]{:T(128)}, f32[8,128,128]{2,1,0:T(8,128)S(1)}, s32[]{:T(128)}, f32[64,8,128,128]{3,2,1,0:T(8,128)}, s32[]{:T(128)}, /*index=5*/s32[]{:T(128)}) while((s32[]{:T(128)}, f32[8,128,128]{2,1,0:T(8,128)S(1)}, s32[]{:T(128)}, f32[64,8,128,128]{3,2,1,0:T(8,128)}, s32[]{:T(128)}, /*index=5*/s32[]{:T(128)}) %tuple.38), condition=%wide.region_1.0_spmd.clone, body=%wide.region_0.0_spmd.clone.sunk | while | flops 393220 | bytes 1572957 | solution.py:28
  158.7 1.2 add_select_fusion.2
  160.0 1.2 add_select_fusion.2
  161.2 1.2 add_select_fusion.2
  162.5 1.2 add_select_fusion.2
  163.7 1.2 add_select_fusion.2
  165.0 1.2 add_select_fusion.2
  166.2 1.2 add_select_fusion.2
  167.5 1.2 add_select_fusion.2
  171.2 1.2 add_select_fusion.2
  172.5 1.2 add_select_fusion.2
  195.0 1.2 add_select_fusion.2
  196.3 1.2 add_select_fusion.2
  218.8 1.2 add_select_fusion.2
  220.1 1.2 add_select_fusion.2
  237.6 2.4 fusion.11
  240.0 5.9 %fusion.5 = (f32[512,8]{0,1:T(8,128)S(1)}, f32[8,128,512]{2,1,0:T(8,128)}) fusion(f32[8,128,512]{2,1,0:T(8,128)} %fusion.11, pred[512,512]{1,0:T(8,128)(4,1)S(1)} %iota_compare_fusion, bf16[512,8,128]{0,2,1:T(8,128)(2,1)S(1)} %bitcast.59, bf16[512,1024]{1,0:T(8,128)(2,1)} %param.9, bf16[512,1024]{1,0:T(8,128)(2,1)S(1)} %copy-done), kind=kOutput, calls=%fused_computation.8 | convolution fusion | flops 1079504896 | bytes 7618560 | tf_op jit(solution)/shard_map/nhqk,nkhd->nqhd/dot_general | solution.py:64
  245.8 1.9 fusion.7
  248.8 52.3 %all_to_all.9 = bf16[512,4,1024]{2,0,1:T(8,128)(2,1)} all-to-all(bf16[512,4,1024]{2,0,1:T(8,128)(2,1)S(1)} %tile.9), channel_id=1, replica_groups=mesh['seq'=64,'fsdp'=4] {'fsdp'}, dimensions={1} | all-to-all | bytes 8388608 | tf_op jit(solution)/shard_map/all_to_all | solution.py:13
  301.1 6.3 %copy.26 = bf16[512,4,1024]{0,2,1:T(8,128)(2,1)} copy(bf16[512,4,1024]{2,0,1:T(8,128)(2,1)} %all_to_all.9) | data formatting | bytes 8388608 | tf_op jit(solution)/shard_map/all_to_all | solution.py:13
  307.3 10.2 %convolution_convert_fusion = bf16[512,1024]{1,0:T(8,128)(2,1)} fusion(bf16[512,4096]{0,1:T(8,128)(2,1)} %bitcast.57, bf16[4096,1024]{1,0:T(8,128)(2,1)} %param.11), kind=kOutput, calls=%fused_computation.12 | convolution fusion | flops 4295491584 | bytes 13631488 | tf_op jit(solution)/shard_map/dot_general | solution.py:70
  (63 shorter events, 62.5 us)
Async XLA Ops:
  6.5 231.0 %copy-start = (bf16[512,1024]{1,0:T(8,128)(2,1)S(1)}, bf16[512,1024]{1,0:T(8,128)(2,1)}, u32[]{:S(2)}) copy-start(bf16[512,1024]{1,0:T(8,128)(2,1)} %param.7) | copy-start | bytes 3145732
  6.5 150.9 %all-gather.3.cloned.1.call-start = ((), (), s32[]{:S(2)}) async-start(), calls=%async_computation.1 | async-start | bytes 34078720 | tf_op jit(solution)/shard_map/all_gather | solution.py:20
  239.9 5.9 %copy-start.2 = (f32[1024]{0:T(1024)S(1)}, f32[1024]{0:T(1024)}, u32[]{:S(2)}) copy-start(f32[1024]{0:T(1024)} %param.10) | copy-start | bytes 12292
  307.3 10.2 %copy-start.1 = (bf16[512,1024]{1,0:T(8,128)(2,1)S(1)}, bf16[512,1024]{1,0:T(8,128)(2,1)}, u32[]{:S(2)}) copy-start(bf16[512,1024]{1,0:T(8,128)(2,1)} %param.7) | copy-start | bytes 3145732
Sparse Core Ops, SparseCore 0:
  10.7 146.6 all-gather.2
